TPU v7x, 32 devices: a whole 2x2x4 slice. The times are simulated.
32 devices in a mesh: row: 16 (over z, y, core), col: 2 (over x).
Axes of the slice: x: 2, y: 2, z: 4, core: 2. Of those that a mesh axis runs over, the one named last changes fastest.
Arguments:
- layer_input: bfloat16 [16384, 1152], P(('row', 'col')), may hold values from -6 to 6
- attn_gain: bfloat16 [1152], replicated, may hold values from 0.099609375 to 1.8984375
- mlp_gain: bfloat16 [1152], replicated, may hold values from 0.099609375 to 1.8984375
- query_weight: bfloat16 [1152, 1152], P('row', 'col'), may hold values from -0.1875 to 0.1875
- key_weight: bfloat16 [1152, 384], P('row', 'col'), may hold values from -0.1875 to 0.1875
- value_weight: bfloat16 [1152, 384], P('row', 'col'), may hold values from -0.1875 to 0.1875
- out_weight: bfloat16 [1152, 1152], P('col', 'row'), may hold values from -4 to 4
- gate_weight: bfloat16 [1152, 3072], P('row', 'col'), may hold values from -0.1875 to 0.1875
- up_weight: bfloat16 [1152, 3072], P('row', 'col'), may hold values from -0.1875 to 0.1875
- down_weight: bfloat16 [3072, 1152], P('col', 'row'), may hold values from -0.109375 to 0.109375
- seq_ids: int32 [16384], P('row'), may hold values from 0 to 31, as said below
- block_ends: int32 [16384], P('row'), may hold values from 255 to 16383, as said below
- grad_output: bfloat16 [16384, 1152], P(('row', 'col')), may hold values from -6 to 6
Outputs:
- layer_output: bfloat16 [16384, 1152], P(('row', 'col'))
- grad_input: bfloat16 [16384, 1152], P(('row', 'col'))
- grad_attn_gain: float32 [1152], replicated
- grad_mlp_gain: float32 [1152], replicated
- grad_query: float32 [1152, 1152], P('row', 'col')
- grad_key: float32 [1152, 384], P('row', 'col')
- grad_value: float32 [1152, 384], P('row', 'col')
- grad_out_weight: float32 [1152, 1152], P('col', 'row')
- grad_gate: float32 [1152, 3072], P('row', 'col')
- grad_up: float32 [1152, 3072], P('row', 'col')
- grad_down: float32 [3072, 1152], P('col', 'row')
Inputs may be any that keep to these rules, and one draw needn't show every extreme that they name: `seq_ids`: ids never fall; span number s of the aligned spans of 1024 tokens holds exactly two sequences, with ids 2 * s and 2 * s + 1, each of 256 tokens or more. `block_ends`: values never fall; an attention block is a run of 1 to 256 tokens inside one sequence, and the first block of every sequence has exactly 256 tokens.
All inputs are finite; a program needn't handle non-finite values.
Results may differ from a plain program's by a relative error of at most 0.014.
The roundings to bfloat16 on the way count: a program that leaves them out, or rounds other values in their place, can miss the bound.
Values may be sent and summed in bfloat16 or wider, within the bound.
A program may use at most 192 MiB of HBM per device.

v0:
```python
import math
import jax
import jax.numpy as jnp
from jax import lax
from jax.sharding import PartitionSpec as P

QUERY_HEADS = 18
KEY_VALUE_HEADS = 6
HEAD_SIZE_DIM = 64
eps = 1e-05
rope_base = 10000.0
neg_fill = -1e30


def rotate_half(values, head_size):
    lane_index = jnp.arange(values.shape[-1], dtype=jnp.int32) % head_size
    forward_roll = jnp.roll(values, -(head_size // 2), axis=-1)
    backward_roll = jnp.roll(values, head_size // 2, axis=-1)
    return jnp.where(lane_index < head_size // 2, -forward_roll, backward_roll)


def rope_tables(position, table_width, head_size):
    lane_index = (jnp.arange(table_width, dtype=jnp.int32) % (head_size // 2)).astype(jnp.float32)
    frequency = jnp.exp(lane_index * (-2.0 * math.log(rope_base) / head_size))
    angles = position[:, None] * frequency[None, :]
    return (jnp.cos(angles), jnp.sin(angles))


def rotary(values, cosine, sine_part, head_size):
    return values * cosine + rotate_half(values, head_size) * sine_part


def rotary_back(upstream, cosine, sine_part, head_size):
    return upstream * cosine - rotate_half(upstream * sine_part, head_size)


def positions(seq_ids):
    token_index = jnp.arange(seq_ids.shape[0], dtype=jnp.int32)
    earlier = jnp.concatenate([seq_ids[:1] - 1, seq_ids[:-1]])
    seq_start = lax.cummax(jnp.where(seq_ids != earlier, token_index, 0), axis=0)
    return (token_index - seq_start).astype(jnp.float32)


def visible(query_seq, query_end, seq_ids, block_ends):
    return (query_seq[:, None] == seq_ids[None, :]) & (block_ends[None, :] <= query_end[:, None])


def to_rows(values):
    return lax.all_to_all(values, "col", split_axis=0, concat_axis=1, tiled=True)


def to_tokens(values):
    return lax.all_to_all(values, "col", split_axis=1, concat_axis=0, tiled=True)


def col_sums(values):
    return lax.psum_scatter(values, "col", scatter_dimension=0, tiled=True)


def widen(values):
    return lax.all_gather(values, "col", axis=0, tiled=True)


def shards(
    layer_input,
    attn_gain,
    mlp_gain,
    query_weight,
    key_weight,
    value_weight,
    out_weight,
    gate_weight,
    up_weight,
    down_weight,
    seq_ids,
    block_ends,
    grad_output,
):
    col_index = lax.axis_index("col")
    query_rows = layer_input.shape[0]
    block_rows = min(512, query_rows)
    block_count = query_rows // block_rows
    heads_per_group = QUERY_HEADS // KEY_VALUE_HEADS
    group_head_width = heads_per_group * HEAD_SIZE_DIM
    query_width = QUERY_HEADS * HEAD_SIZE_DIM
    score_scale = HEAD_SIZE_DIM ** (-0.5)
    attn_gain_float = attn_gain.astype(jnp.float32)
    mlp_gain_float = mlp_gain.astype(jnp.float32)
    full_input = lax.all_gather(layer_input, "col", axis=0, tiled=True)
    token_rows = full_input.shape[0]
    query_cols, key_cols, value_cols, out_rows, gate_cols, up_cols, down_rows = (
        lax.all_gather(query_weight, "row", axis=0, tiled=True),
        lax.all_gather(key_weight, "row", axis=0, tiled=True),
        lax.all_gather(value_weight, "row", axis=0, tiled=True),
        lax.all_gather(out_weight, "row", axis=1, tiled=True),
        lax.all_gather(gate_weight, "row", axis=0, tiled=True),
        lax.all_gather(up_weight, "row", axis=0, tiled=True),
        lax.all_gather(down_weight, "row", axis=1, tiled=True),
    )
    input_float = full_input.astype(jnp.float32)
    inv_all = lax.rsqrt(jnp.mean(input_float * input_float, axis=1, keepdims=True) + eps)
    attn_in = (input_float * inv_all * attn_gain_float).astype(jnp.bfloat16)
    query_unrotated = jnp.dot(attn_in, query_cols, preferred_element_type=jnp.float32).astype(
        jnp.bfloat16
    )
    key_raw = jnp.dot(attn_in, key_cols, preferred_element_type=jnp.float32).astype(jnp.bfloat16)
    value_projected = jnp.dot(attn_in, value_cols, preferred_element_type=jnp.float32).astype(
        jnp.bfloat16
    )
    query_all = to_rows(query_unrotated)
    key_all, value_all = (
        lax.all_gather(key_raw, "col", axis=1, tiled=True),
        lax.all_gather(value_projected, "col", axis=1, tiled=True),
    )
    position = positions(seq_ids)
    row_start = col_index * query_rows
    query_pos = lax.dynamic_slice_in_dim(position, row_start, query_rows)
    query_seq = lax.dynamic_slice_in_dim(seq_ids, row_start, query_rows)
    query_end = lax.dynamic_slice_in_dim(block_ends, row_start, query_rows)
    query_cos, query_sin = rope_tables(query_pos, query_width, HEAD_SIZE_DIM)
    key_cos, key_sin = rope_tables(position, key_all.shape[1], HEAD_SIZE_DIM)
    query_rotated = (
        rotary(query_all.astype(jnp.float32), query_cos, query_sin, HEAD_SIZE_DIM) * score_scale
    ).astype(jnp.bfloat16)
    key_rotated = rotary(key_all.astype(jnp.float32), key_cos, key_sin, HEAD_SIZE_DIM).astype(
        jnp.bfloat16
    )

    def block_inputs(block_index):
        first_row = block_index * block_rows
        allowed = visible(query_seq, query_end, seq_ids, block_ends)
        return (first_row, allowed)

    def group_scores(query_block, group_index, allowed):
        query_head_rows = lax.dynamic_slice_in_dim(
            query_block, group_index * group_head_width, group_head_width, 1
        ).reshape(block_rows, heads_per_group, HEAD_SIZE_DIM)
        key_group = lax.dynamic_slice_in_dim(
            key_rotated, group_index * HEAD_SIZE_DIM, HEAD_SIZE_DIM, 1
        )
        value_group = lax.dynamic_slice_in_dim(
            value_all, group_index * HEAD_SIZE_DIM, HEAD_SIZE_DIM, 1
        )
        scores = jnp.einsum(
            "qhd,kd->hqk", query_head_rows, key_group, preferred_element_type=jnp.float32
        )
        return (query_head_rows, key_group, value_group, jnp.where(allowed[None], scores, neg_fill))

    def attend_block(block_index):
        first_row, allowed = block_inputs(block_index)

        def attend_head_group(group_index):
            query_head_rows, key_group, value_group, scores = group_scores(
                query_rotated, group_index, allowed
            )
            row_top = jnp.max(scores, axis=2, keepdims=True)
            powers = jnp.exp(scores - row_top)
            exp_total = jnp.sum(powers, axis=2, keepdims=True)
            attn_probs = (powers / exp_total).astype(jnp.bfloat16)
            weighted_values = jnp.einsum(
                "hqk,kd->qhd", attn_probs, value_group, preferred_element_type=jnp.float32
            )
            return (
                weighted_values.reshape(block_rows, group_head_width),
                (row_top + jnp.log(exp_total))[:, :, 0],
            )

        weighted_value_rows, logsumexp_rows = lax.map(
            attend_head_group, jnp.arange(KEY_VALUE_HEADS, dtype=jnp.int32)
        )
        return (
            jnp.transpose(weighted_value_rows, (1, 0, 2)).reshape(block_rows, query_width),
            logsumexp_rows,
        )

    mixed_blocks, log_blocks = lax.map(attend_block, jnp.arange(block_count, dtype=jnp.int32))
    attn_rows = mixed_blocks.reshape(query_rows, query_width).astype(jnp.bfloat16)
    attn_tokens = to_tokens(attn_rows)
    attn_share = col_sums(jnp.dot(attn_tokens, out_rows, preferred_element_type=jnp.float32))
    residual = layer_input.astype(jnp.float32) + attn_share
    inv_two = lax.rsqrt(jnp.mean(residual * residual, axis=1, keepdims=True) + eps)
    normed_two = residual * inv_two
    mlp_in = widen((normed_two * mlp_gain_float).astype(jnp.bfloat16))
    gate_act = jnp.dot(mlp_in, gate_cols, preferred_element_type=jnp.float32)
    up_act = jnp.dot(mlp_in, up_cols, preferred_element_type=jnp.float32)
    hidden = (jax.nn.silu(gate_act) * up_act).astype(jnp.bfloat16)
    mlp_share = col_sums(jnp.dot(hidden, down_rows, preferred_element_type=jnp.float32))
    layer_output = (residual + mlp_share).astype(jnp.bfloat16)
    grad_float = grad_output.astype(jnp.float32)
    grad_full = widen(grad_output)
    grad_down = jnp.einsum("tf,td->fd", hidden, grad_full, preferred_element_type=jnp.float32)
    grad_hidden = jnp.einsum("td,fd->tf", grad_full, down_rows, preferred_element_type=jnp.float32)
    gate_sigmoid = jax.nn.sigmoid(gate_act)
    grad_gate_act = (
        grad_hidden * up_act * gate_sigmoid * (1.0 + gate_act * (1.0 - gate_sigmoid))
    ).astype(jnp.bfloat16)
    grad_up_act = (grad_hidden * gate_act * gate_sigmoid).astype(jnp.bfloat16)
    grad_gate = jnp.einsum("td,tf->df", mlp_in, grad_gate_act, preferred_element_type=jnp.float32)
    grad_up = jnp.einsum("td,tf->df", mlp_in, grad_up_act, preferred_element_type=jnp.float32)
    grad_mlp_share = col_sums(
        jnp.einsum("tf,df->td", grad_gate_act, gate_cols, preferred_element_type=jnp.float32)
        + jnp.einsum("tf,df->td", grad_up_act, up_cols, preferred_element_type=jnp.float32)
    )
    scaled_two = grad_mlp_share * mlp_gain_float
    inner_two = jnp.mean(scaled_two * normed_two, axis=1, keepdims=True)
    grad_residual = grad_float + inv_two * (scaled_two - normed_two * inner_two)
    grad_mlp_gain = jnp.sum(grad_mlp_share * normed_two, axis=0)
    grad_branch = grad_residual.astype(jnp.bfloat16)
    grad_attn_full = widen(grad_branch)
    grad_out_weight = jnp.einsum(
        "tq,td->qd", attn_tokens, grad_attn_full, preferred_element_type=jnp.float32
    )
    grad_mixture = to_rows(
        jnp.einsum(
            "td,qd->tq", grad_attn_full, out_rows, preferred_element_type=jnp.float32
        ).astype(jnp.bfloat16)
    )

    def back_block(carried_state, scan_items):
        block_index, block_log_total = scan_items
        first_row, allowed = block_inputs(block_index)

        def backward_head_group(inner_acc, group_items):
            group_index, log_group = group_items
            keys_acc, values_acc = inner_acc
            query_head_rows, key_group, value_group, scores = group_scores(
                query_rotated, group_index, allowed
            )
            attn_probs = jnp.exp(scores - log_group[:, :, None])
            grad_heads = lax.dynamic_slice_in_dim(
                grad_mixture, group_index * group_head_width, group_head_width, 1
            ).reshape(block_rows, heads_per_group, HEAD_SIZE_DIM)
            grad_probs = jnp.einsum(
                "qhd,kd->hqk", grad_heads, value_group, preferred_element_type=jnp.float32
            )
            value_piece = jnp.einsum(
                "hqk,qhd->kd",
                attn_probs.astype(jnp.bfloat16),
                grad_heads,
                preferred_element_type=jnp.float32,
            )
            inner_dot = jnp.sum(attn_probs * grad_probs, axis=2, keepdims=True)
            grad_scores = (attn_probs * (grad_probs - inner_dot)).astype(jnp.bfloat16)
            query_piece = jnp.einsum(
                "hqk,kd->qhd", grad_scores, key_group, preferred_element_type=jnp.float32
            ).reshape(block_rows, group_head_width)
            key_piece = jnp.einsum(
                "hqk,qhd->kd", grad_scores, query_head_rows, preferred_element_type=jnp.float32
            )
            column = group_index * HEAD_SIZE_DIM
            keys_acc = lax.dynamic_update_slice_in_dim(
                keys_acc,
                lax.dynamic_slice_in_dim(keys_acc, column, HEAD_SIZE_DIM, 1) + key_piece,
                column,
                1,
            )
            values_acc = lax.dynamic_update_slice_in_dim(
                values_acc,
                lax.dynamic_slice_in_dim(values_acc, column, HEAD_SIZE_DIM, 1) + value_piece,
                column,
                1,
            )
            return ((keys_acc, values_acc), query_piece)

        carried_state, query_pieces = lax.scan(
            backward_head_group,
            carried_state,
            (jnp.arange(KEY_VALUE_HEADS, dtype=jnp.int32), block_log_total),
        )
        return (
            carried_state,
            jnp.transpose(query_pieces, (1, 0, 2)).reshape(block_rows, query_width),
        )

    zeros_kv = jnp.zeros((token_rows, key_all.shape[1]), jnp.float32)
    (grad_keys, grad_values), query_blocks = lax.scan(
        back_block, (zeros_kv, zeros_kv), (jnp.arange(block_count, dtype=jnp.int32), log_blocks)
    )
    grad_query_rot = query_blocks.reshape(query_rows, query_width)
    grad_query_raw = to_tokens(
        rotary_back(grad_query_rot * score_scale, query_cos, query_sin, HEAD_SIZE_DIM).astype(
            jnp.bfloat16
        )
    )
    grad_key_part = rotary_back(grad_keys, key_cos, key_sin, HEAD_SIZE_DIM)
    grad_key_sum, grad_value_sum = (
        lax.psum_scatter(grad_key_part, "col", scatter_dimension=1, tiled=True),
        lax.psum_scatter(grad_values, "col", scatter_dimension=1, tiled=True),
    )
    grad_key_raw = grad_key_sum.astype(jnp.bfloat16)
    grad_value_raw = grad_value_sum.astype(jnp.bfloat16)
    grad_query = jnp.einsum(
        "td,tq->dq", attn_in, grad_query_raw, preferred_element_type=jnp.float32
    )
    grad_key = jnp.einsum("td,tq->dq", attn_in, grad_key_raw, preferred_element_type=jnp.float32)
    grad_value = jnp.einsum(
        "td,tq->dq", attn_in, grad_value_raw, preferred_element_type=jnp.float32
    )
    grad_attn_share = col_sums(
        jnp.einsum("tq,dq->td", grad_query_raw, query_cols, preferred_element_type=jnp.float32)
        + jnp.einsum("tq,dq->td", grad_key_raw, key_cols, preferred_element_type=jnp.float32)
        + jnp.einsum("tq,dq->td", grad_value_raw, value_cols, preferred_element_type=jnp.float32)
    )
    own_float = layer_input.astype(jnp.float32)
    inv_one = lax.rsqrt(jnp.mean(own_float * own_float, axis=1, keepdims=True) + eps)
    normed_one = own_float * inv_one
    scaled_one = grad_attn_share * attn_gain_float
    inner_one = jnp.mean(scaled_one * normed_one, axis=1, keepdims=True)
    grad_input = (grad_residual + inv_one * (scaled_one - normed_one * inner_one)).astype(
        jnp.bfloat16
    )
    grad_attn_gain = jnp.sum(grad_attn_share * normed_one, axis=0)
    weight_sums = (
        lax.psum_scatter(grad_query, "row", scatter_dimension=0, tiled=True),
        lax.psum_scatter(grad_key, "row", scatter_dimension=0, tiled=True),
        lax.psum_scatter(grad_value, "row", scatter_dimension=0, tiled=True),
        lax.psum_scatter(grad_out_weight, "row", scatter_dimension=1, tiled=True),
        lax.psum_scatter(grad_gate, "row", scatter_dimension=0, tiled=True),
        lax.psum_scatter(grad_up, "row", scatter_dimension=0, tiled=True),
        lax.psum_scatter(grad_down, "row", scatter_dimension=1, tiled=True),
    )
    gain_sums = lax.psum((grad_attn_gain, grad_mlp_gain), ("row", "col"))
    return (
        layer_output,
        grad_input,
        gain_sums[0],
        gain_sums[1],
        weight_sums[0],
        weight_sums[1],
        weight_sums[2],
        weight_sums[3],
        weight_sums[4],
        weight_sums[5],
        weight_sums[6],
    )


def solution(mesh):
    in_specs = (
        P(("row", "col"), None),
        P(),
        P(),
        P("row", "col"),
        P("row", "col"),
        P("row", "col"),
        P("col", "row"),
        P("row", "col"),
        P("row", "col"),
        P("col", "row"),
        P("row"),
        P("row"),
        P(("row", "col"), None),
    )
    out_specs = (
        P(("row", "col"), None),
        P(("row", "col"), None),
        P(),
        P(),
        P("row", "col"),
        P("row", "col"),
        P("row", "col"),
        P("col", "row"),
        P("row", "col"),
        P("row", "col"),
        P("col", "row"),
    )
    return jax.shard_map(shards, mesh=mesh, in_specs=in_specs, out_specs=out_specs, check_vma=False)
```

profile of v0, /device:TPU:0, one launch (start us, length us, event | category | flops | bytes accessed | tf_op | source)
XLA Modules:
  0.0 1523.2 jit_solution(14034235379282888117)
XLA Ops:
  14.5 24.8 %all_gather.42 = bf16[1152,192]{1,0:T(8,128)(2,1)S(1)} all-gather(bf16[72,192]{1,0:T(8,128)(2,1)S(1)} %copy-done.33), channel_id=1, replica_groups=mesh['row'=16,'col'=2] {'row'}, dimensions={0}, use_global_device_ids=true | all-gather | bytes 470016 | tf_op jit(solution)/shard_map/all_gather | solution.py:93
  39.4 19.0 %all_gather.40 = bf16[1152,192]{1,0:T(8,128)(2,1)S(1)} all-gather(bf16[72,192]{1,0:T(8,128)(2,1)S(1)} %copy-done.34), channel_id=1, replica_groups=mesh['row'=16,'col'=2] {'row'}, dimensions={0}, use_global_device_ids=true | all-gather | bytes 470016 | tf_op jit(solution)/shard_map/all_gather | solution.py:94
  62.2 12.0 all_gather.43
  76.2 11.4 all_gather.41
  115.5 11.3 fusion.64
  126.8 62.2 %while.50 = (s32[]{:T(128)}, bf16[6,512,192]{1,2,0:T(8,128)(2,1)S(1)}, f32[6,3,512]{2,1,0:T(4,128)}, s32[6]{0:T(128)S(1)}, bf16[1024,384]{0,1:T(8,128)(2,1)}, /*...) while((s32[]{:T(128)}, ...), condition=%wide.region_6.7_spmd.clone.clone, body=%wide.region_3.6_spmd.clone.sunk.clone | while | flops 418380288 | bytes 22477056 | solution.py:168
  189.0 17.3 %all_to_all.64 = bf16[512,2,576]{0,2,1:T(8,128)(2,1)S(1)} all-to-all(bf16[512,2,576]{0,2,1:T(8,128)(2,1)S(1)} %bitcast.276), channel_id=1, replica_groups=mesh['row'=16,'col'=2] {'col'}, dimensions={1} | all-to-all | bytes 2359296 | tf_op jit(solution)/shard_map/all_to_all | solution.py:53
  214.1 56.8 %reduce-scatter.18.cloned.1.call-done = f32[512,1152]{1,0:T(8,128)} async-done(((f32[1024,1152]{1,0:T(8,128)}), f32[512,1152]{1,0:T(8,128)}) %reduce-scatter.18.cloned.1.call-update) | async-done | bytes 2359312 | tf_op jit(solution)/shard_map/reduce_scatter | solution.py:57
  277.9 42.6 %all-gather.20.cloned.1.call-done = bf16[1152,1536]{1,0:T(8,128)(2,1)} async-done(((bf16[72,1536]{1,0:T(8,128)(2,1)}), bf16[1152,1536]{1,0:T(8,128)(2,1)}) %all-gather.20.cloned.1.call-update) | async-done | bytes 3538960 | tf_op jit(solution)/shard_map/all_gather | solution.py:97
  320.5 37.1 %all-gather.16.cloned.1.call-done = bf16[1024,1152]{1,0:T(8,128)(2,1)} async-done(((bf16[512,1152]{1,0:T(8,128)(2,1)}), bf16[1024,1152]{1,0:T(8,128)(2,1)}) %all-gather.16.cloned.1.call-update) | async-done | bytes 2359312 | tf_op jit(solution)/shard_map/all_gather | solution.py:61
  357.6 9.6 fusion.126
  367.3 40.2 %all-gather.18.cloned.1.call-done = bf16[1152,1536]{1,0:T(8,128)(2,1)} async-done(((bf16[72,1536]{1,0:T(8,128)(2,1)}), bf16[1152,1536]{1,0:T(8,128)(2,1)}) %all-gather.18.cloned.1.call-update) | async-done | bytes 3538960 | tf_op jit(solution)/shard_map/all_gather | solution.py:96
  407.4 9.7 fusion.125
  417.1 27.0 %all-gather.24.cloned.1.call-done = bf16[1024,1152]{1,0:T(8,128)(2,1)} async-done(((bf16[512,1152]{1,0:T(8,128)(2,1)}), bf16[1024,1152]{1,0:T(8,128)(2,1)}) %all-gather.24.cloned.1.call-update) | async-done | bytes 2359312 | tf_op jit(solution)/shard_map/all_gather | solution.py:61
  444.1 49.8 %all-gather.22.cloned.1.call-done = bf16[1536,1152]{0,1:T(8,128)(2,1)} async-done(((bf16[1536,72]{0,1:T(8,128)(2,1)}), bf16[1536,1152]{0,1:T(8,128)(2,1)}) %all-gather.22.cloned.1.call-update) | async-done | bytes 3538960 | tf_op jit(solution)/shard_map/all_gather | solution.py:98
  493.9 12.5 multiply_convert_fusion
  516.8 59.1 %reduce-scatter.22.cloned.1.call-done = f32[512,1152]{1,0:T(8,128)} async-done(((f32[1024,1152]{1,0:T(8,128)}), f32[512,1152]{1,0:T(8,128)}) %reduce-scatter.22.cloned.1.call-update) | async-done | bytes 2359312 | tf_op jit(solution)/shard_map/reduce_scatter | solution.py:57
  581.8 36.2 %all-gather.26.cloned.1.call-done = bf16[1024,1152]{1,0:T(8,128)(2,1)} async-done(((bf16[512,1152]{1,0:T(8,128)(2,1)}), bf16[1024,1152]{1,0:T(8,128)(2,1)}) %all-gather.26.cloned.1.call-update) | async-done | bytes 2359312 | tf_op jit(solution)/shard_map/all_gather | solution.py:61
  627.7 15.1 all-to-all-done.2
  645.5 125.0 %while.51 = (s32[]{:T(128)}, f32[1024,384]{0,1:T(8,128)}, f32[1024,384]{0,1:T(8,128)}, f32[6,512,192]{1,2,0:T(8,128)}, s32[6]{0:T(128)S(1)}, /*index=5*/bf16[102...) while((s32[]{:T(128)}, f32[1024,384]{0,1:T(8,128)}, ...), condition=%wide.region_15.16_spmd.clone.clone, body=%wide.region_13.15_spmd.clone.sunk.clone | while | flops 1027209728 | bytes 55630144 | solution.py:265
  796.7 8.7 subtract_convert_fusion
  805.4 18.5 %all_to_all.65 = bf16[512,2,576]{0,2,1:T(8,128)(2,1)S(1)} all-to-all(bf16[512,2,576]{0,2,1:T(8,128)(2,1)S(1)} %subtract_convert_fusion), channel_id=1, replica_groups=mesh['row'=16,'col'=2] {'col'}, dimensions={1} | all-to-all | bytes 2359296 | tf_op jit(solution)/shard_map/all_to_all | solution.py:53
  846.7 9.4 fusion.127
  909.8 40.1 %all-reduce.2 = (f32[1152]{0:T(1024)}, f32[1152]{0:T(1024)}) all-reduce(f32[1152]{0:T(1024)} %get-tuple-element.251, f32[1152]{0:T(1024)} %get-tuple-element.249), channel_id=1, replica_groups=mesh['row'=16,'col'=2] {'row','col'}, use_global_device_ids=true, to_apply=%region_21.22 | all-reduce | flops 2304 | bytes 18432 | tf_op jit(solution)/shard_map/psum | solution.py:322
  951.1 19.2 %reduce-scatter.20.cloned.1.call-done = f32[512,1152]{1,0:T(8,128)} async-done(((f32[1024,1152]{1,0:T(8,128)}), f32[512,1152]{1,0:T(8,128)}) %reduce-scatter.20.cloned.1.call-update) | async-done | bytes 2359312 | tf_op jit(solution)/shard_map/reduce_scatter | solution.py:57
  975.4 89.2 %reduce-scatter.38.cloned.1.call-done = f32[1536,72]{0,1:T(8,128)} async-done(((f32[1536,1152]{0,1:T(8,128)}), f32[1536,72]{0,1:T(8,128)}) %reduce-scatter.38.cloned.1.call-update) | async-done | bytes 442384 | tf_op jit(solution)/shard_map/reduce_scatter | solution.py:320
  1064.7 94.5 %reduce-scatter.36.cloned.1.call-done = f32[72,1536]{1,0:T(8,128)} async-done(((f32[1152,1536]{1,0:T(8,128)}), f32[72,1536]{1,0:T(8,128)}) %reduce-scatter.36.cloned.1.call-update) | async-done | bytes 442384 | tf_op jit(solution)/shard_map/reduce_scatter | solution.py:319
  1159.2 94.0 %reduce-scatter.34.cloned.1.call-done = f32[72,1536]{1,0:T(8,128)} async-done(((f32[1152,1536]{1,0:T(8,128)}), f32[72,1536]{1,0:T(8,128)}) %reduce-scatter.34.cloned.1.call-update) | async-done | bytes 442384 | tf_op jit(solution)/shard_map/reduce_scatter | solution.py:318
  1253.3 69.9 %reduce-scatter.42.cloned.1.call-done = f32[576,72]{0,1:T(8,128)} async-done(((f32[576,1152]{0,1:T(8,128)}), f32[576,72]{0,1:T(8,128)}) %reduce-scatter.42.cloned.1.call-update) | async-done | bytes 165904
  1323.1 61.6 %reduce-scatter.32.cloned.1.call-done = f32[72,192]{1,0:T(8,128)} async-done(((f32[1152,192]{1,0:T(8,128)}), f32[72,192]{1,0:T(8,128)}) %reduce-scatter.32.cloned.1.call-update) | async-done | bytes 55312 | tf_op jit(solution)/shard_map/reduce_scatter | solution.py:316
  1384.8 61.8 %reduce-scatter.30.cloned.1.call-done = f32[72,192]{1,0:T(8,128)} async-done(((f32[1152,192]{1,0:T(8,128)}), f32[72,192]{1,0:T(8,128)}) %reduce-scatter.30.cloned.1.call-update) | async-done | bytes 55312 | tf_op jit(solution)/shard_map/reduce_scatter | solution.py:315
  1446.6 69.3 %reduce-scatter.40.cloned.1.call-done = f32[72,576]{1,0:T(8,128)} async-done(((f32[1152,576]{1,0:T(8,128)}), f32[72,576]{1,0:T(8,128)}) %reduce-scatter.40.cloned.1.call-update) | async-done | bytes 165904
  (358 shorter events, 363.0 us)
Async XLA Ops:
  7.2 51.2 %all-gather.10.cloned.1.call-start = ((), (), s32[]{:S(2)}) async-start(), calls=%async_computation.17 | async-start | bytes 3538944 | tf_op jit(solution)/shard_map/all_gather | solution.py:89
  8.0 82.0 %all-gather.12.cloned.1.call-start = ((), (), s32[]{:S(2)}) async-start(), calls=%async_computation.18 | async-start | bytes 1566720 | tf_op jit(solution)/shard_map/all_gather | solution.py:92
  8.7 197.8 %all-gather.14.cloned.1.call-start = ((), (), s32[]{:S(2)}) async-start(), calls=%async_computation.19 | async-start | bytes 1566720 | tf_op jit(solution)/shard_map/all_gather | solution.py:95
  13.9 47.0 %copy-start.24 = (f32[1024]{0:T(1024)}, f32[1024]{0:T(1024)S(1)}, u32[]{:S(2)}) copy-start(f32[1024]{0:T(1024)S(1)} %fusion.97) | copy-start | bytes 12292
  95.1 19.3 %all-to-all-start = ((bf16[2,512,576]{1,2,0:T(8,128)(2,1)}), bf16[2,512,576]{1,2,0:T(8,128)(2,1)S(1)}, u32[]{:S(2)}, u32[]{:S(2)}) async-start(bf16[2,512,576]{1,2,0:T(8,128)(2,1)} %bitcast.277), calls=%async_computation | async-start | bytes 2359296 | tf_op jit(solution)/shard_map/all_to_all | solution.py:49
  98.7 172.2 %reduce-scatter.18.cloned.1.call-start = ((), (), s32[]{:S(2)}) async-start(), calls=%async_computation.20 | async-start | bytes 7077888 | tf_op jit(solution)/shard_map/reduce_scatter | solution.py:57
  212.8 58.1 %copy-start.7 = (bf16[512,1152]{1,0:T(8,128)(2,1)S(1)}, bf16[512,1152]{1,0:T(8,128)(2,1)}, u32[]{:S(2)}) copy-start(bf16[512,1152]{1,0:T(8,128)(2,1)} %param.17) | copy-start | bytes 3538948
  212.8 107.7 %all-gather.20.cloned.1.call-start = ((), (), s32[]{:S(2)}) async-start(), calls=%async_computation.23 | async-start | bytes 3760128 | tf_op jit(solution)/shard_map/all_gather | solution.py:97
  213.4 144.2 %all-gather.16.cloned.1.call-start = ((), (), s32[]{:S(2)}) async-start(), calls=%async_computation.21 | async-start | bytes 3538944 | tf_op jit(solution)/shard_map/all_gather | solution.py:61
  273.7 305.2 %copy-start.1 = (f32[512,1152]{1,0:T(8,128)}, f32[512,1152]{1,0:T(8,128)S(1)}, u32[]{:S(2)}) copy-start(f32[512,1152]{1,0:T(8,128)S(1)} %get-tuple-element.306) | copy-start | bytes 7077892
  275.3 132.2 %all-gather.18.cloned.1.call-start = ((), (), s32[]{:S(2)}) async-start(), calls=%async_computation.22 | async-start | bytes 3760128 | tf_op jit(solution)/shard_map/all_gather | solution.py:96
  276.0 168.1 %all-gather.24.cloned.1.call-start = ((), (), s32[]{:S(2)}) async-start(), calls=%async_computation.26 | async-start | bytes 3538944 | tf_op jit(solution)/shard_map/all_gather | solution.py:61
  276.8 217.1 %all-gather.22.cloned.1.call-start = ((), (), s32[]{:S(2)}) async-start(), calls=%async_computation.24 | async-start | bytes 3760128 | tf_op jit(solution)/shard_map/all_gather | solution.py:98
  277.5 298.4 %reduce-scatter.22.cloned.1.call-start = ((), (), s32[]{:S(2)}) async-start(), calls=%async_computation.27 | async-start | bytes 7077888 | tf_op jit(solution)/shard_map/reduce_scatter | solution.py:57
  516.7 62.8 %copy-start.9 = (bf16[512,1152]{1,0:T(8,128)(2,1)S(1)}, bf16[512,1152]{1,0:T(8,128)(2,1)}, u32[]{:S(2)}) copy-start(bf16[512,1152]{1,0:T(8,128)(2,1)} %param.29) | copy-start | bytes 3538948
  516.7 101.3 %all-gather.26.cloned.1.call-start = ((), (), s32[]{:S(2)}) async-start(), calls=%async_computation.28 | async-start | bytes 3538944 | tf_op jit(solution)/shard_map/all_gather | solution.py:61
  623.0 19.8 %all-to-all-start.2 = ((bf16[2,512,576]{1,2,0:T(8,128)(2,1)}), bf16[2,512,576]{1,2,0:T(8,128)(2,1)}, u32[]{:S(2)}, u32[]{:S(2)}) async-start(bf16[2,512,576]{1,2,0:T(8,128)(2,1)} %bitcast.162), calls=%async_computation.5 | async-start | bytes 2359296 | tf_op jit(solution)/shard_map/all_to_all | solution.py:49
  627.4 201.0 %reduce-scatter.24.cloned.1.call-start = ((), (), s32[]{:S(2)}) async-start(), calls=%async_computation.29 | async-start | bytes 2359296 | tf_op jit(solution)/shard_map/reduce_scatter | solution.py:287
  645.5 125.0 %copy-start.26 = (f32[1024]{0:T(1024)S(1)}, f32[1024]{0:T(1024)}, u32[]{:S(2)}) copy-start(f32[1024]{0:T(1024)} %copy-done.24) | copy-start | bytes 12292
  645.5 125.0 %copy-start.36 = (f32[384]{0:T(512)S(1)}, f32[384]{0:T(512)}, u32[]{:S(2)}) copy-start(f32[384]{0:T(512)} %fusion.100) | copy-start | bytes 4612
  785.3 55.7 %reduce-scatter.26.cloned.1.call-start = ((), (), s32[]{:S(2)}) async-start(), calls=%async_computation.30 | async-start | bytes 2359296 | tf_op jit(solution)/shard_map/reduce_scatter | solution.py:288
  794.4 112.4 %reduce-scatter.28.cloned.1.call-start = ((), (), s32[]{:S(2)}) async-start(), calls=%async_computation.31 | async-start | bytes 7077888 | tf_op jit(solution)/shard_map/reduce_scatter | solution.py:57
  846.7 123.7 %reduce-scatter.20.cloned.1.call-start = ((), (), s32[]{:S(2)}) async-start(), calls=%async_computation.25 | async-start | bytes 7077888 | tf_op jit(solution)/shard_map/reduce_scatter | solution.py:57
  856.1 208.6 %reduce-scatter.38.cloned.1.call-start = ((), (), s32[]{:S(2)}) async-start(), calls=%async_computation.36 | async-start | bytes 7520256 | tf_op jit(solution)/shard_map/reduce_scatter | solution.py:320
  865.4 293.8 %reduce-scatter.36.cloned.1.call-start = ((), (), s32[]{:S(2)}) async-start(), calls=%async_computation.35 | async-start | bytes 7520256 | tf_op jit(solution)/shard_map/reduce_scatter | solution.py:319
  874.7 378.6 %reduce-scatter.34.cloned.1.call-start = ((), (), s32[]{:S(2)}) async-start(), calls=%async_computation.34 | async-start | bytes 7520256 | tf_op jit(solution)/shard_map/reduce_scatter | solution.py:318
  882.6 440.5 %reduce-scatter.42.cloned.1.call-start = ((), (), s32[]{:S(2)}) async-start(), calls=%async_computation.38 | async-start | bytes 3133440
  889.3 495.4 %reduce-scatter.32.cloned.1.call-start = ((), (), s32[]{:S(2)}) async-start(), calls=%async_computation.33 | async-start | bytes 1253376 | tf_op jit(solution)/shard_map/reduce_scatter | solution.py:316
  894.2 552.4 %reduce-scatter.30.cloned.1.call-start = ((), (), s32[]{:S(2)}) async-start(), calls=%async_computation.32 | async-start | bytes 1253376 | tf_op jit(solution)/shard_map/reduce_scatter | solution.py:315
  897.5 618.4 %reduce-scatter.40.cloned.1.call-start = ((), (), s32[]{:S(2)}) async-start(), calls=%async_computation.37 | async-start | bytes 3133440
  901.6 68.7 %copy-start.2 = (f32[512,1152]{1,0:T(8,128)S(1)}, f32[512,1152]{1,0:T(8,128)}, u32[]{:S(2)}) copy-start(f32[512,1152]{1,0:T(8,128)} %copy-done.1) | copy-start | bytes 7077892
  901.6 68.7 %copy-start.23 = (f32[1152]{0:T(1024)S(1)}, f32[1152]{0:T(1024)}, u32[]{:S(2)}) copy-start(f32[1152]{0:T(1024)} %convert_element_type.142) | copy-start | bytes 13828
  (51 other events, 326.2 us)
Sparse Core Ops, SparseCore 0:
  9.6 38.7 all-gather.9
  50.6 39.3 all-gather.11
  92.1 38.1 all-gather.13
  212.9 57.8 reduce-scatter.17
  273.3 47.1 all-gather.19
  322.5 35.0 all-gather.15
  360.2 47.1 all-gather.17
  409.0 35.0 all-gather.23
  446.7 47.1 all-gather.21
  516.8 58.9 reduce-scatter.21
  582.0 36.0 all-gather.25
  785.4 26.4 reduce-scatter.23
  814.2 26.7 reduce-scatter.25
  846.8 59.9 reduce-scatter.27
  909.1 61.2 reduce-scatter.19
  974.8 89.8 reduce-scatter.37
  1069.6 89.5 reduce-scatter.35
  1163.7 89.5 reduce-scatter.33
  1258.3 64.8 reduce-scatter.41
  1327.6 57.0 reduce-scatter.31
  1389.4 57.1 reduce-scatter.29
  1451.6 64.2 reduce-scatter.39
where the time goes:
time: 1530 us; the launch traced here: 1520 us
  waiting for transfers between devices  949 us (62%)
  matrix products  228 us (15%)
  blocking collectives  143 us (9%)
  other arithmetic  115 us (8%)
  local copies, waits for them, and re-layouts  45.7 us (3%)
  loops' own time  16.1 us (1%)
  between operations  16.1 us (1%)
    unnamed x24, waiting for transfers between devices  144 us
    reduce_scatter x4, waiting for transfers between devices, col_sums(): return lax.psum_scatter(values, 'col', scatter_dimension=0, tiled=True)  139 us
    all_gather x3, waiting for transfers between devices, widen(): return lax.all_gather(values, 'col', axis=0, tiled=True)  100 us
    reduce_scatter x1, waiting for transfers between devices, shards(): lax.psum_scatter(grad_up, 'row', scatter_dimension=0, tiled=True)  94.5 us
    reduce_scatter x1, waiting for transfers between devices, shards(): lax.psum_scatter(grad_gate, 'row', scatter_dimension=0, tiled=True)  94 us
    reduce_scatter x1, waiting for transfers between devices, shards(): lax.psum_scatter(grad_down, 'row', scatter_dimension=1, tiled=True)  89.2 us
    reduce_scatter x1, waiting for transfers between devices, shards(): lax.psum_scatter(grad_key, 'row', scatter_dimension=0, tiled=True)  61.8 us
    reduce_scatter x1, waiting for transfers between devices, shards(): lax.psum_scatter(grad_value, 'row', scatter_dimension=0, tiled=True)  61.6 us
  transfers between devices with their start and end apart: 24, of which 21 were waited for; matrix products, arithmetic and copies ran while one was open for 13% of the time, Pallas kernels for 0%

commit v1 on v0

--- a/solution.py
+++ b/solution.py
@@ -319,7 +319,9 @@
         lax.psum_scatter(grad_up, "row", scatter_dimension=0, tiled=True),
         lax.psum_scatter(grad_down, "row", scatter_dimension=1, tiled=True),
     )
-    gain_sums = lax.psum((grad_attn_gain, grad_mlp_gain), ("row", "col"))
+    gain_sums = (grad_attn_gain, grad_mlp_gain)
+    for over in ("col", "row"):
+        gain_sums = lax.psum(gain_sums, over)
     return (
         layer_output,
         grad_input,

time: 1530 us -> 1530 us (level)
  waiting for transfers between devices: 949 us -> 920 us
  blocking collectives: 143 us -> 171 us
    psum x1 -> x2, blocking collectives: 40.1 us -> 67.7 us  [shards(): gain_sums = lax.psum(gain_sums, over)]
    reduce_scatter x4, waiting for transfers between devices: 139 us -> 120 us  [col_sums(): return lax.psum_scatter(values, 'col', scatter_dimension=0, tiled=True)]
  transfers between devices with their start and end apart: 24 -> 24, of which waited for: 21 -> 20; matrix products, arithmetic and copies ran while one was open for 13% -> 13% of each run, Pallas kernels for 0% -> 0%
where the time goes in v1:
time: 1530 us; the launch traced here: 1520 us
  waiting for transfers between devices  920 us (60%)
  matrix products  227 us (15%)
  blocking collectives  171 us (11%)
  other arithmetic  116 us (8%)
  local copies, waits for them, and re-layouts  45.6 us (3%)
  loops' own time  16.1 us (1%)
  between operations  16.1 us (1%)
    unnamed x24, waiting for transfers between devices  144 us
    reduce_scatter x4, waiting for transfers between devices, col_sums(): return lax.psum_scatter(values, 'col', scatter_dimension=0, tiled=True)  120 us
    all_gather x3, waiting for transfers between devices, widen(): return lax.all_gather(values, 'col', axis=0, tiled=True)  100 us
    reduce_scatter x1, waiting for transfers between devices, shards(): lax.psum_scatter(grad_up, 'row', scatter_dimension=0, tiled=True)  94.6 us
    reduce_scatter x1, waiting for transfers between devices, shards(): lax.psum_scatter(grad_gate, 'row', scatter_dimension=0, tiled=True)  94 us
    reduce_scatter x1, waiting for transfers between devices, shards(): lax.psum_scatter(grad_down, 'row', scatter_dimension=1, tiled=True)  79.3 us
    psum x2, blocking collectives, shards(): gain_sums = lax.psum(gain_sums, over)  67.7 us
    reduce_scatter x1, waiting for transfers between devices, shards(): lax.psum_scatter(grad_key, 'row', scatter_dimension=0, tiled=True)  61.7 us
  transfers between devices with their start and end apart: 24, of which 20 were waited for; matrix products, arithmetic and copies ran while one was open for 13% of the time, Pallas kernels for 0%

profile of v1, /device:TPU:0, one launch (start us, length us, event | category | flops | bytes accessed | tf_op | source)
XLA Modules:
  0.0 1521.9 jit_solution(14098197420800026804)
XLA Ops:
  14.5 24.8 %all_gather.42 = bf16[1152,192]{1,0:T(8,128)(2,1)S(1)} all-gather(bf16[72,192]{1,0:T(8,128)(2,1)S(1)} %copy-done.33), channel_id=1, replica_groups=mesh['row'=16,'col'=2] {'row'}, dimensions={0}, use_global_device_ids=true | all-gather | bytes 470016 | tf_op jit(solution)/shard_map/all_gather | solution.py:93
  39.4 19.0 %all_gather.40 = bf16[1152,192]{1,0:T(8,128)(2,1)S(1)} all-gather(bf16[72,192]{1,0:T(8,128)(2,1)S(1)} %copy-done.34), channel_id=1, replica_groups=mesh['row'=16,'col'=2] {'row'}, dimensions={0}, use_global_device_ids=true | all-gather | bytes 470016 | tf_op jit(solution)/shard_map/all_gather | solution.py:94
  62.2 12.0 all_gather.43
  76.2 11.4 all_gather.41
  115.5 11.3 fusion.64
  126.8 62.2 %while.50 = (s32[]{:T(128)}, bf16[6,512,192]{1,2,0:T(8,128)(2,1)S(1)}, f32[6,3,512]{2,1,0:T(4,128)}, s32[6]{0:T(128)S(1)}, bf16[1024,384]{0,1:T(8,128)(2,1)}, /*...) while((s32[]{:T(128)}, ...), condition=%wide.region_6.7_spmd.clone.clone, body=%wide.region_3.6_spmd.clone.sunk.clone | while | flops 418380288 | bytes 22477056 | solution.py:168
  189.0 17.3 %all_to_all.64 = bf16[512,2,576]{0,2,1:T(8,128)(2,1)S(1)} all-to-all(bf16[512,2,576]{0,2,1:T(8,128)(2,1)S(1)} %bitcast.276), channel_id=1, replica_groups=mesh['row'=16,'col'=2] {'col'}, dimensions={1} | all-to-all | bytes 2359296 | tf_op jit(solution)/shard_map/all_to_all | solution.py:53
  214.1 56.8 %reduce-scatter.18.cloned.1.call-done = f32[512,1152]{1,0:T(8,128)} async-done(((f32[1024,1152]{1,0:T(8,128)}), f32[512,1152]{1,0:T(8,128)}) %reduce-scatter.18.cloned.1.call-update) | async-done | bytes 2359312 | tf_op jit(solution)/shard_map/reduce_scatter | solution.py:57
  277.9 42.6 %all-gather.20.cloned.1.call-done = bf16[1152,1536]{1,0:T(8,128)(2,1)} async-done(((bf16[72,1536]{1,0:T(8,128)(2,1)}), bf16[1152,1536]{1,0:T(8,128)(2,1)}) %all-gather.20.cloned.1.call-update) | async-done | bytes 3538960 | tf_op jit(solution)/shard_map/all_gather | solution.py:97
  320.5 37.1 %all-gather.16.cloned.1.call-done = bf16[1024,1152]{1,0:T(8,128)(2,1)} async-done(((bf16[512,1152]{1,0:T(8,128)(2,1)}), bf16[1024,1152]{1,0:T(8,128)(2,1)}) %all-gather.16.cloned.1.call-update) | async-done | bytes 2359312 | tf_op jit(solution)/shard_map/all_gather | solution.py:61
  357.6 9.6 fusion.126
  367.2 40.2 %all-gather.18.cloned.1.call-done = bf16[1152,1536]{1,0:T(8,128)(2,1)} async-done(((bf16[72,1536]{1,0:T(8,128)(2,1)}), bf16[1152,1536]{1,0:T(8,128)(2,1)}) %all-gather.18.cloned.1.call-update) | async-done | bytes 3538960 | tf_op jit(solution)/shard_map/all_gather | solution.py:96
  407.4 9.7 fusion.125
  417.1 27.0 %all-gather.24.cloned.1.call-done = bf16[1024,1152]{1,0:T(8,128)(2,1)} async-done(((bf16[512,1152]{1,0:T(8,128)(2,1)}), bf16[1024,1152]{1,0:T(8,128)(2,1)}) %all-gather.24.cloned.1.call-update) | async-done | bytes 2359312 | tf_op jit(solution)/shard_map/all_gather | solution.py:61
  444.1 49.8 %all-gather.22.cloned.1.call-done = bf16[1536,1152]{0,1:T(8,128)(2,1)} async-done(((bf16[1536,72]{0,1:T(8,128)(2,1)}), bf16[1536,1152]{0,1:T(8,128)(2,1)}) %all-gather.22.cloned.1.call-update) | async-done | bytes 3538960 | tf_op jit(solution)/shard_map/all_gather | solution.py:98
  493.9 12.4 multiply_convert_fusion
  516.7 59.1 %reduce-scatter.22.cloned.1.call-done = f32[512,1152]{1,0:T(8,128)} async-done(((f32[1024,1152]{1,0:T(8,128)}), f32[512,1152]{1,0:T(8,128)}) %reduce-scatter.22.cloned.1.call-update) | async-done | bytes 2359312 | tf_op jit(solution)/shard_map/reduce_scatter | solution.py:57
  581.6 36.3 %all-gather.26.cloned.1.call-done = bf16[1024,1152]{1,0:T(8,128)(2,1)} async-done(((bf16[512,1152]{1,0:T(8,128)(2,1)}), bf16[1024,1152]{1,0:T(8,128)(2,1)}) %all-gather.26.cloned.1.call-update) | async-done | bytes 2359312 | tf_op jit(solution)/shard_map/all_gather | solution.py:61
  627.5 15.1 all-to-all-done.2
  645.3 125.1 %while.51 = (s32[]{:T(128)}, f32[1024,384]{0,1:T(8,128)}, f32[1024,384]{0,1:T(8,128)}, f32[6,512,192]{1,2,0:T(8,128)}, s32[6]{0:T(128)S(1)}, /*index=5*/bf16[102...) while((s32[]{:T(128)}, f32[1024,384]{0,1:T(8,128)}, ...), condition=%wide.region_15.16_spmd.clone.clone, body=%wide.region_13.15_spmd.clone.sunk.clone | while | flops 1027209728 | bytes 55630144 | solution.py:265
  796.5 8.7 subtract_convert_fusion
  805.2 18.5 %all_to_all.65 = bf16[512,2,576]{0,2,1:T(8,128)(2,1)S(1)} all-to-all(bf16[512,2,576]{0,2,1:T(8,128)(2,1)S(1)} %subtract_convert_fusion), channel_id=1, replica_groups=mesh['row'=16,'col'=2] {'col'}, dimensions={1} | all-to-all | bytes 2359296 | tf_op jit(solution)/shard_map/all_to_all | solution.py:53
  846.5 9.4 fusion.127
  909.6 8.2 all-reduce.3
  917.8 59.5 %all-reduce.2 = (f32[1152]{0:T(1024)}, f32[1152]{0:T(1024)}) all-reduce(f32[1152]{0:T(1024)} %get-tuple-element.305, f32[1152]{0:T(1024)} %get-tuple-element.306), channel_id=1, replica_groups=mesh['row'=16,'col'=2] {'row'}, use_global_device_ids=true, to_apply=%region_22.23 | all-reduce | flops 2304 | bytes 18432 | tf_op jit(solution)/shard_map/psum | solution.py:324
  984.2 79.3 %reduce-scatter.38.cloned.1.call-done = f32[1536,72]{0,1:T(8,128)} async-done(((f32[1536,1152]{0,1:T(8,128)}), f32[1536,72]{0,1:T(8,128)}) %reduce-scatter.38.cloned.1.call-update) | async-done | bytes 442384 | tf_op jit(solution)/shard_map/reduce_scatter | solution.py:320
  1063.5 94.6 %reduce-scatter.36.cloned.1.call-done = f32[72,1536]{1,0:T(8,128)} async-done(((f32[1152,1536]{1,0:T(8,128)}), f32[72,1536]{1,0:T(8,128)}) %reduce-scatter.36.cloned.1.call-update) | async-done | bytes 442384 | tf_op jit(solution)/shard_map/reduce_scatter | solution.py:319
  1158.1 94.0 %reduce-scatter.34.cloned.1.call-done = f32[72,1536]{1,0:T(8,128)} async-done(((f32[1152,1536]{1,0:T(8,128)}), f32[72,1536]{1,0:T(8,128)}) %reduce-scatter.34.cloned.1.call-update) | async-done | bytes 442384 | tf_op jit(solution)/shard_map/reduce_scatter | solution.py:318
  1252.1 69.8 %reduce-scatter.42.cloned.1.call-done = f32[576,72]{0,1:T(8,128)} async-done(((f32[576,1152]{0,1:T(8,128)}), f32[576,72]{0,1:T(8,128)}) %reduce-scatter.42.cloned.1.call-update) | async-done | bytes 165904
  1321.9 61.6 %reduce-scatter.32.cloned.1.call-done = f32[72,192]{1,0:T(8,128)} async-done(((f32[1152,192]{1,0:T(8,128)}), f32[72,192]{1,0:T(8,128)}) %reduce-scatter.32.cloned.1.call-update) | async-done | bytes 55312 | tf_op jit(solution)/shard_map/reduce_scatter | solution.py:316
  1383.6 61.7 %reduce-scatter.30.cloned.1.call-done = f32[72,192]{1,0:T(8,128)} async-done(((f32[1152,192]{1,0:T(8,128)}), f32[72,192]{1,0:T(8,128)}) %reduce-scatter.30.cloned.1.call-update) | async-done | bytes 55312 | tf_op jit(solution)/shard_map/reduce_scatter | solution.py:315
  1445.3 69.3 %reduce-scatter.40.cloned.1.call-done = f32[72,576]{1,0:T(8,128)} async-done(((f32[1152,576]{1,0:T(8,128)}), f32[72,576]{1,0:T(8,128)}) %reduce-scatter.40.cloned.1.call-update) | async-done | bytes 165904
  (359 shorter events, 363.4 us)
Async XLA Ops:
  7.2 51.2 %all-gather.10.cloned.1.call-start = ((), (), s32[]{:S(2)}) async-start(), calls=%async_computation.17 | async-start | bytes 3538944 | tf_op jit(solution)/shard_map/all_gather | solution.py:89
  8.0 82.0 %all-gather.12.cloned.1.call-start = ((), (), s32[]{:S(2)}) async-start(), calls=%async_computation.18 | async-start | bytes 1566720 | tf_op jit(solution)/shard_map/all_gather | solution.py:92
  8.7 197.8 %all-gather.14.cloned.1.call-start = ((), (), s32[]{:S(2)}) async-start(), calls=%async_computation.19 | async-start | bytes 1566720 | tf_op jit(solution)/shard_map/all_gather | solution.py:95
  13.9 47.0 %copy-start.24 = (f32[1024]{0:T(1024)}, f32[1024]{0:T(1024)S(1)}, u32[]{:S(2)}) copy-start(f32[1024]{0:T(1024)S(1)} %fusion.97) | copy-start | bytes 12292
  95.1 19.3 %all-to-all-start = ((bf16[2,512,576]{1,2,0:T(8,128)(2,1)}), bf16[2,512,576]{1,2,0:T(8,128)(2,1)S(1)}, u32[]{:S(2)}, u32[]{:S(2)}) async-start(bf16[2,512,576]{1,2,0:T(8,128)(2,1)} %bitcast.277), calls=%async_computation | async-start | bytes 2359296 | tf_op jit(solution)/shard_map/all_to_all | solution.py:49
  98.7 172.2 %reduce-scatter.18.cloned.1.call-start = ((), (), s32[]{:S(2)}) async-start(), calls=%async_computation.20 | async-start | bytes 7077888 | tf_op jit(solution)/shard_map/reduce_scatter | solution.py:57
  212.8 58.1 %copy-start.7 = (bf16[512,1152]{1,0:T(8,128)(2,1)S(1)}, bf16[512,1152]{1,0:T(8,128)(2,1)}, u32[]{:S(2)}) copy-start(bf16[512,1152]{1,0:T(8,128)(2,1)} %param.17) | copy-start | bytes 3538948
  212.8 107.7 %all-gather.20.cloned.1.call-start = ((), (), s32[]{:S(2)}) async-start(), calls=%async_computation.23 | async-start | bytes 3760128 | tf_op jit(solution)/shard_map/all_gather | solution.py:97
  213.4 144.2 %all-gather.16.cloned.1.call-start = ((), (), s32[]{:S(2)}) async-start(), calls=%async_computation.21 | async-start | bytes 3538944 | tf_op jit(solution)/shard_map/all_gather | solution.py:61
  273.7 305.0 %copy-start.1 = (f32[512,1152]{1,0:T(8,128)}, f32[512,1152]{1,0:T(8,128)S(1)}, u32[]{:S(2)}) copy-start(f32[512,1152]{1,0:T(8,128)S(1)} %get-tuple-element.308) | copy-start | bytes 7077892
  275.2 132.2 %all-gather.18.cloned.1.call-start = ((), (), s32[]{:S(2)}) async-start(), calls=%async_computation.22 | async-start | bytes 3760128 | tf_op jit(solution)/shard_map/all_gather | solution.py:96
  276.0 168.1 %all-gather.24.cloned.1.call-start = ((), (), s32[]{:S(2)}) async-start(), calls=%async_computation.26 | async-start | bytes 3538944 | tf_op jit(solution)/shard_map/all_gather | solution.py:61
  276.7 217.1 %all-gather.22.cloned.1.call-start = ((), (), s32[]{:S(2)}) async-start(), calls=%async_computation.24 | async-start | bytes 3760128 | tf_op jit(solution)/shard_map/all_gather | solution.py:98
  277.5 298.2 %reduce-scatter.22.cloned.1.call-start = ((), (), s32[]{:S(2)}) async-start(), calls=%async_computation.27 | async-start | bytes 7077888 | tf_op jit(solution)/shard_map/reduce_scatter | solution.py:57
  516.6 62.7 %copy-start.9 = (bf16[512,1152]{1,0:T(8,128)(2,1)S(1)}, bf16[512,1152]{1,0:T(8,128)(2,1)}, u32[]{:S(2)}) copy-start(bf16[512,1152]{1,0:T(8,128)(2,1)} %param.29) | copy-start | bytes 3538948
  516.6 101.3 %all-gather.26.cloned.1.call-start = ((), (), s32[]{:S(2)}) async-start(), calls=%async_computation.28 | async-start | bytes 3538944 | tf_op jit(solution)/shard_map/all_gather | solution.py:61
  622.8 19.8 %all-to-all-start.2 = ((bf16[2,512,576]{1,2,0:T(8,128)(2,1)}), bf16[2,512,576]{1,2,0:T(8,128)(2,1)}, u32[]{:S(2)}, u32[]{:S(2)}) async-start(bf16[2,512,576]{1,2,0:T(8,128)(2,1)} %bitcast.162), calls=%async_computation.5 | async-start | bytes 2359296 | tf_op jit(solution)/shard_map/all_to_all | solution.py:49
  627.2 201.0 %reduce-scatter.24.cloned.1.call-start = ((), (), s32[]{:S(2)}) async-start(), calls=%async_computation.29 | async-start | bytes 2359296 | tf_op jit(solution)/shard_map/reduce_scatter | solution.py:287
  645.3 125.1 %copy-start.26 = (f32[1024]{0:T(1024)S(1)}, f32[1024]{0:T(1024)}, u32[]{:S(2)}) copy-start(f32[1024]{0:T(1024)} %copy-done.24) | copy-start | bytes 12292
  645.3 125.1 %copy-start.36 = (f32[384]{0:T(512)S(1)}, f32[384]{0:T(512)}, u32[]{:S(2)}) copy-start(f32[384]{0:T(512)} %fusion.100) | copy-start | bytes 4612
  785.1 55.7 %reduce-scatter.26.cloned.1.call-start = ((), (), s32[]{:S(2)}) async-start(), calls=%async_computation.30 | async-start | bytes 2359296 | tf_op jit(solution)/shard_map/reduce_scatter | solution.py:288
  794.2 112.4 %reduce-scatter.28.cloned.1.call-start = ((), (), s32[]{:S(2)}) async-start(), calls=%async_computation.31 | async-start | bytes 7077888 | tf_op jit(solution)/shard_map/reduce_scatter | solution.py:57
  846.4 132.1 %reduce-scatter.20.cloned.1.call-start = ((), (), s32[]{:S(2)}) async-start(), calls=%async_computation.25 | async-start | bytes 7077888 | tf_op jit(solution)/shard_map/reduce_scatter | solution.py:57
  855.9 207.6 %reduce-scatter.38.cloned.1.call-start = ((), (), s32[]{:S(2)}) async-start(), calls=%async_computation.36 | async-start | bytes 7520256 | tf_op jit(solution)/shard_map/reduce_scatter | solution.py:320
  865.2 292.8 %reduce-scatter.36.cloned.1.call-start = ((), (), s32[]{:S(2)}) async-start(), calls=%async_computation.35 | async-start | bytes 7520256 | tf_op jit(solution)/shard_map/reduce_scatter | solution.py:319
  874.5 377.6 %reduce-scatter.34.cloned.1.call-start = ((), (), s32[]{:S(2)}) async-start(), calls=%async_computation.34 | async-start | bytes 7520256 | tf_op jit(solution)/shard_map/reduce_scatter | solution.py:318
  882.4 439.5 %reduce-scatter.42.cloned.1.call-start = ((), (), s32[]{:S(2)}) async-start(), calls=%async_computation.38 | async-start | bytes 3133440
  889.1 494.5 %reduce-scatter.32.cloned.1.call-start = ((), (), s32[]{:S(2)}) async-start(), calls=%async_computation.33 | async-start | bytes 1253376 | tf_op jit(solution)/shard_map/reduce_scatter | solution.py:316
  894.0 551.4 %reduce-scatter.30.cloned.1.call-start = ((), (), s32[]{:S(2)}) async-start(), calls=%async_computation.32 | async-start | bytes 1253376 | tf_op jit(solution)/shard_map/reduce_scatter | solution.py:315
  897.3 617.3 %reduce-scatter.40.cloned.1.call-start = ((), (), s32[]{:S(2)}) async-start(), calls=%async_computation.37 | async-start | bytes 3133440
  901.3 77.2 %copy-start.2 = (f32[512,1152]{1,0:T(8,128)S(1)}, f32[512,1152]{1,0:T(8,128)}, u32[]{:S(2)}) copy-start(f32[512,1152]{1,0:T(8,128)} %copy-done.1) | copy-start | bytes 7077892
  901.3 77.2 %copy-start.23 = (f32[1152]{0:T(1024)S(1)}, f32[1152]{0:T(1024)}, u32[]{:S(2)}) copy-start(f32[1152]{0:T(1024)} %convert_element_type.142) | copy-start | bytes 13828
  (51 other events, 325.9 us)
Sparse Core Ops, SparseCore 0:
  9.6 38.7 all-gather.9
  50.6 39.3 all-gather.11
  92.1 38.1 all-gather.13
  212.9 57.8 reduce-scatter.17
  273.3 47.1 all-gather.19
  322.5 35.0 all-gather.15
  360.2 47.1 all-gather.17
  409.0 35.0 all-gather.23
  446.7 47.1 all-gather.21
  516.7 58.9 reduce-scatter.21
  581.7 36.0 all-gather.25
  785.2 26.4 reduce-scatter.23
  814.0 26.7 reduce-scatter.25
  846.6 59.9 reduce-scatter.27
  908.9 60.0 reduce-scatter.19
  973.4 90.0 reduce-scatter.37
  1068.5 89.5 reduce-scatter.35
  1162.5 89.5 reduce-scatter.33
  1257.1 64.7 reduce-scatter.41
  1326.4 57.1 reduce-scatter.31
  1388.2 57.0 reduce-scatter.29
  1450.3 64.2 reduce-scatter.39
